TPU v7x, 128 devices: a whole 4x4x4 slice. The times are simulated.
128 devices in a mesh: dp: 16 (over y, x), expert: 4 (over z), tensor: 2 (over core).
Axes of the slice: x: 4, y: 4, z: 4, core: 2. Of those that a mesh axis runs over, the one named last changes fastest.
Arguments:
- tokens: bfloat16 [8192, 2048], P(('dp', 'expert')), may hold values from -6 to 6
- expert_ids: int32 [8192, 2], P(('dp', 'expert')), may hold values from 0 to 3, all different within a row; in each aligned block of 128 rows (0 to 127, 128 to 255, ...) at most 96 rows name the same one
- gate_values: float32 [8192, 2], P(('dp', 'expert')), may hold values from 0.1 to 1
- tag_labels: int32 [8192], P(('dp', 'expert')), may hold values from 0 to 31
- w_gate: bfloat16 [4, 2048, 7168], P('expert', 'dp', 'tensor'), may hold values from -0.125 to 0.125
- w_up: bfloat16 [4, 2048, 7168], P('expert', 'dp', 'tensor'), may hold values from -0.125 to 0.125
- w_down: bfloat16 [4, 7168, 2048], P('expert', 'tensor', 'dp'), may hold values from -0.0625 to 0.0625
- adapter_in: bfloat16 [4, 16, 2048], P('expert'), may hold values from -0.125 to 0.125
- adapter_out: bfloat16 [4, 16, 7168], P('expert', None, 'tensor'), may hold values from -1.5 to 1.5
- tag_weight: bfloat16 [2048, 32], replicated, may hold values from -0.125 to 0.125
Outputs:
- layer_out: bfloat16 [8192, 2048], P(('dp', 'expert'), 'tensor')
- in_gradient: float32 [4, 16, 2048], P('expert')
- out_gradient: float32 [4, 16, 7168], P('expert', None, 'tensor')
Inputs may be any that keep to these rules, and one draw needn't show every extreme that they name: `expert_ids`: each row names 2 different experts; the rows of one index of dp and expert name each expert at most 96 times, a bound that some block reaches.
All inputs are finite; a program needn't handle non-finite values.
Results may differ from a plain program's by a relative error of at most 0.017.
Values may be sent and summed in bfloat16 or wider, within the bound.
A program may use at most 128 MiB of HBM per device.

v0:
```python
import jax
import jax.numpy as jnp
from jax import lax
from jax.sharding import PartitionSpec as P

adapter_scale = 2.0


def contract_last(left, right):
    return lax.dot_general(
        left, right, (((1,), (1,)), ((), ())), preferred_element_type=jnp.float32
    )


def contract_first(left, right):
    return lax.dot_general(
        left, right, (((0,), (0,)), ((), ())), preferred_element_type=jnp.float32
    )


def tag_gradient(logits, tag_labels):
    exp_logits = jnp.exp(logits)
    probability = exp_logits / jnp.sum(exp_logits, axis=1, keepdims=True)
    labels_hot = (
        tag_labels[:, None] == jnp.arange(logits.shape[1], dtype=jnp.int32)[None, :]
    ).astype(jnp.float32)
    return probability - labels_hot


def local(
    tokens,
    expert_ids,
    gate_values,
    tag_labels,
    w_gate,
    w_up,
    w_down,
    adapter_in,
    adapter_out,
    tag_weight,
):
    experts = lax.axis_size("expert")
    shards = lax.axis_size("tensor")
    tok_count = tokens.shape[0]
    model_width = tokens.shape[1]
    share_width = model_width // shards
    capacity = 3 * tok_count // experts
    slot_count = experts * capacity
    flat_ids = expert_ids.reshape(-1)
    onehot = (flat_ids[:, None] == jnp.arange(experts, dtype=jnp.int32)[None, :]).astype(jnp.int32)
    before = jnp.cumsum(onehot, axis=0) - onehot
    position = jnp.sum(before * onehot, axis=1)
    slot_index = (flat_ids * capacity + position).reshape(tok_count, expert_ids.shape[1])
    matches = jnp.arange(slot_count, dtype=jnp.int32)[:, None, None] == slot_index[None, :, :]
    dispatch = jnp.sum(matches.astype(jnp.float32), axis=2).astype(jnp.bfloat16)
    combine = jnp.sum(jnp.where(matches, gate_values[None, :, :], jnp.float32(0.0)), axis=2).T
    outgoing = jnp.dot(dispatch, tokens, preferred_element_type=jnp.float32).astype(jnp.bfloat16)
    arrived = lax.all_to_all(
        outgoing.reshape(experts, capacity, model_width),
        "expert",
        split_axis=0,
        concat_axis=0,
        tiled=True,
    ).reshape(slot_count, model_width)
    gate_acc = jnp.dot(
        arrived,
        lax.all_gather(w_gate, "dp", axis=1, tiled=True)[0],
        preferred_element_type=jnp.float32,
    )
    up_acc = jnp.dot(
        arrived,
        lax.all_gather(w_up, "dp", axis=1, tiled=True)[0],
        preferred_element_type=jnp.float32,
    )
    low_rank = contract_last(arrived, adapter_in[0]).astype(jnp.bfloat16)
    up_full = up_acc + adapter_scale * jnp.dot(
        low_rank, adapter_out[0], preferred_element_type=jnp.float32
    )
    activated = jax.nn.silu(gate_acc)
    hidden = (activated * up_full).astype(jnp.bfloat16)
    down_full = lax.all_gather(w_down, "dp", axis=2, tiled=True)[0]
    partial_value = jnp.dot(hidden, down_full, preferred_element_type=jnp.float32)
    column_start = lax.axis_index("tensor") * share_width
    summed = lax.psum(partial_value, "tensor").astype(jnp.bfloat16)
    returned = lax.all_to_all(
        summed.reshape(experts, capacity, model_width),
        "expert",
        split_axis=0,
        concat_axis=0,
        tiled=True,
    ).reshape(slot_count, model_width)
    mixed_rows = tokens.astype(jnp.float32) + jnp.dot(
        combine, returned.astype(jnp.float32), precision=lax.Precision.HIGHEST
    )
    layer_full = mixed_rows.astype(jnp.bfloat16)
    logits = jnp.dot(layer_full, tag_weight, preferred_element_type=jnp.float32)
    logit_grad = tag_gradient(logits, tag_labels)
    upstream = jnp.dot(
        logit_grad, tag_weight.astype(jnp.float32).T, precision=lax.Precision.HIGHEST
    )
    slot_out = jnp.dot(combine.T, upstream, precision=lax.Precision.HIGHEST).astype(jnp.bfloat16)
    slot_grad = lax.all_to_all(
        slot_out.reshape(experts, capacity, model_width),
        "expert",
        split_axis=0,
        concat_axis=0,
        tiled=True,
    ).reshape(slot_count, model_width)
    layer_out = lax.dynamic_slice_in_dim(layer_full, column_start, share_width, 1)
    hidden_grad = contract_last(slot_grad, down_full)
    up_grad = (hidden_grad * activated).astype(jnp.bfloat16)
    out_local = adapter_scale * contract_first(low_rank, up_grad)
    low_grad = adapter_scale * contract_last(up_grad, adapter_out[0])
    in_local = lax.dot_general(
        low_grad,
        arrived.astype(jnp.float32),
        (((0,), (0,)), ((), ())),
        precision=lax.Precision.HIGHEST,
    )
    in_total = lax.psum(in_local.astype(jnp.bfloat16), ("dp", "tensor")).astype(jnp.float32)
    out_total = lax.psum(out_local.astype(jnp.bfloat16), "dp").astype(jnp.float32)
    return (layer_out, in_total[None], out_total[None])


def solution(mesh):
    in_specs = (
        P(("dp", "expert"), None),
        P(("dp", "expert"), None),
        P(("dp", "expert"), None),
        P(("dp", "expert")),
        P("expert", "dp", "tensor"),
        P("expert", "dp", "tensor"),
        P("expert", "tensor", "dp"),
        P("expert", None, None),
        P("expert", None, "tensor"),
        P(),
    )
    out_specs = (
        P(("dp", "expert"), "tensor"),
        P("expert", None, None),
        P("expert", None, "tensor"),
    )
    return jax.shard_map(local, mesh=mesh, in_specs=in_specs, out_specs=out_specs, check_vma=False)
```

profile of v0, /device:TPU:0, one launch (start us, length us, event | category | flops | bytes accessed | tf_op | source)
XLA Modules:
  0.0 610.8 jit_solution(16985919612496595279)
XLA Ops:
  7.2 0.0 all-gather.6.cloned.1.call-start
  7.2 0.7 all-gather.6.cloned.1.call-update
  7.9 0.0 all-gather.4.cloned.1.call-start
  8.0 0.7 all-gather.4.cloned.1.call-update
  8.7 0.0 all-gather.8.cloned.1.call-start
  8.7 0.7 all-gather.8.cloned.1.call-update
  9.4 0.8 copy.31
  10.2 0.1 eq.56
  10.4 0.1 eq.52
  10.5 1.2 reduce-window.6
  11.8 0.1 slice.8
  11.8 0.1 copy.33
  12.0 0.1 copy.34
  12.1 0.1 add_bitcast_fusion
  12.2 0.1 reduce_sum.39
  12.3 0.1 copy.35
  12.4 0.7 multiply_add_fusion
  13.1 0.8 convert_reduce_fusion
  13.9 0.6 convolution_convert_fusion.1
  14.4 25.9 %all_to_all.15 = bf16[4,96,2048]{2,1,0:T(8,128)(2,1)S(1)} all-to-all(bf16[4,96,2048]{2,1,0:T(8,128)(2,1)S(1)} %bitcast.78), channel_id=1, replica_groups=mesh['dp'=16,'expert'=4,'tensor'=2] {'expert'}, dimensions={0} | all-to-all | bytes 3145728 | tf_op jit(solution)/shard_map/all_to_all | solution.py:58
  40.4 0.5 convolution_convert_fusion.3
  40.9 72.1 %all-gather.6.cloned.1.call-done = bf16[1,2048,3584]{2,1,0:T(8,128)(2,1)} async-done(((bf16[1,128,3584]{2,1,0:T(8,128)(2,1)}), bf16[1,2048,3584]{2,1,0:T(8,128)(2,1)}) %all-gather.6.cloned.1.call-update) | async-done | bytes 14680080 | tf_op jit(solution)/shard_map/all_gather | solution.py:72
  113.0 11.5 %fusion.4 = f32[384,3584]{1,0:T(8,128)} fusion(bf16[384,2048]{1,0:T(8,128)(2,1)S(1)} %bitcast.75, bf16[1,2048,3584]{2,1,0:T(8,128)(2,1)} %all-gather.6.cloned.1.call-done), kind=kOutput, calls=%fused_computation.4 | convolution fusion | flops 5637144576 | bytes 21757952 | tf_op jit(solution)/shard_map/dot_general | solution.py:70
  124.5 90.7 %all-gather.4.cloned.1.call-done = bf16[1,2048,3584]{2,1,0:T(8,128)(2,1)} async-done(((bf16[1,128,3584]{2,1,0:T(8,128)(2,1)}), bf16[1,2048,3584]{2,1,0:T(8,128)(2,1)}) %all-gather.4.cloned.1.call-update) | async-done | bytes 14680080 | tf_op jit(solution)/shard_map/all_gather | solution.py:67
  215.2 11.1 %divide_multiply_fusion = f32[384,3584]{1,0:T(8,128)} fusion(bf16[384,2048]{1,0:T(8,128)(2,1)S(1)} %bitcast.76, bf16[1,2048,3584]{2,1,0:T(8,128)(2,1)} %all-gather.4.cloned.1.call-done), kind=kOutput, calls=%fused_computation.14 | convolution fusion | flops 5642649600 | bytes 21757952 | tf_op jit(solution)/shard_map/dot_general | solution.py:65
  226.4 99.8 %all-gather.8.cloned.1.call-done = bf16[1,3584,2048]{2,1,0:T(8,128)(2,1)} async-done(((bf16[1,3584,128]{2,1,0:T(8,128)(2,1)}), bf16[1,3584,2048]{2,1,0:T(8,128)(2,1)}) %all-gather.8.cloned.1.call-update) | async-done | bytes 14680080 | tf_op jit(solution)/shard_map/all_gather | solution.py:81
  326.1 15.2 %fusion.2 = f32[384,2048]{1,0:T(8,128)} fusion(bf16[1,3584,2048]{2,1,0:T(8,128)(2,1)} %all-gather.8.cloned.1.call-done, f32[384,3584]{1,0:T(8,128)} %divide_multiply_fusion, f32[384,3584]{1,0:T(8,128)} %fusion.4, bf16[384,16]{0,1:T(8,128)(2,1)S(1)} %convolution_convert_fusion.3, bf16[1,16,3584]{2,1,0:T(8,128)(2,1)S(1)} %copy-done.4), kind=kOutput, calls=%fused_computation.2 | convolution fusion | flops 5686689792 | bytes 28962816 | tf_op jit(solution)/shard_map/dot_general | solution.py:82
  341.3 12.2 %all-reduce.7 = bf16[384,2048]{1,0:T(8,128)(2,1)S(1)} all-reduce(f32[384,2048]{1,0:T(8,128)} %fusion.2), channel_id=1, replica_groups=mesh['dp'=16,'expert'=4,'tensor'=2] {'tensor'}, use_global_device_ids=true, to_apply=%region_5.6 | all-reduce | flops 786432 | bytes 4718592 | tf_op jit(solution)/shard_map/psum | solution.py:84
  353.6 25.5 %all_to_all.16 = bf16[4,96,2048]{2,1,0:T(8,128)(2,1)S(1)} all-to-all(bf16[4,96,2048]{2,1,0:T(8,128)(2,1)S(1)} %bitcast.80), channel_id=1, replica_groups=mesh['dp'=16,'expert'=4,'tensor'=2] {'expert'}, dimensions={0} | all-to-all | bytes 3145728 | tf_op jit(solution)/shard_map/all_to_all | solution.py:85
  379.0 1.0 fusion.21
  380.1 0.3 fusion.38
  380.4 0.6 fusion.28
  381.0 3.7 convolution_convert_fusion
  384.8 4.4 all-to-all-start.2
  389.1 0.0 all-reduce.4.cloned.1.call-start
  389.2 20.4 %all-to-all-done.2 = bf16[4,96,2048]{2,1,0:T(8,128)(2,1)} async-done(((bf16[4,96,2048]{2,1,0:T(8,128)(2,1)}), bf16[4,96,2048]{2,1,0:T(8,128)(2,1)}, u32[]{:S(2)}, u32[]{:S(2)}) %all-to-all-start.2) | async-done | bytes 1572896 | tf_op jit(solution)/shard_map/all_to_all | solution.py:102
  409.6 10.4 %fusion.13 = bf16[384,3584]{1,0:T(8,128)(2,1)S(1)} fusion(f32[384,3584]{1,0:T(8,128)} %divide_multiply_fusion, bf16[384,2048]{1,0:T(8,128)(2,1)} %bitcast.12, bf16[1,3584,2048]{2,1,0:T(8,128)(2,1)} %all-gather.8.cloned.1.call-done), kind=kOutput, calls=%fused_computation.12 | convolution fusion | flops 5639897088 | bytes 24510464 | tf_op jit(solution)/shard_map/dot_general | solution.py:10
  420.0 0.8 convolution_multiply_fusion.2
  420.9 0.6 copy-done.2
  421.4 1.4 fusion.22
  422.8 0.0 all-reduce.4.cloned.1.call-update
  422.8 0.0 all-reduce.6.cloned.1.call-start
  422.9 1.1 fusion.20
  424.0 0.7 constant_dynamic-slice_fusion
  424.7 92.3 %all-reduce.4.cloned.1.call-done = bf16[1,16,2048]{2,1,0:T(8,128)(2,1)} async-done(((bf16[1,16,2048]{2,1,0:T(8,128)(2,1)}), bf16[1,16,2048]{2,1,0:T(8,128)(2,1)}) %all-reduce.4.cloned.1.call-update) | async-done | bytes 65552 | tf_op jit(solution)/shard_map/psum | solution.py:120
  517.0 1.5 broadcast_in_dim.33
  518.5 84.1 %all-reduce.6.cloned.1.call-done = bf16[1,16,3584]{2,1,0:T(8,128)(2,1)} async-done(((bf16[1,16,3584]{2,1,0:T(8,128)(2,1)}), bf16[1,16,3584]{2,1,0:T(8,128)(2,1)}) %all-reduce.6.cloned.1.call-update) | async-done | bytes 114704 | tf_op jit(solution)/shard_map/psum | solution.py:121
  602.7 1.6 broadcast_in_dim.35
  (18 shorter events, 0.1 us)
Async XLA Ops:
  7.2 372.9 %copy-start = (bf16[2048,32]{0,1:T(8,128)(2,1)S(1)}, bf16[2048,32]{0,1:T(8,128)(2,1)}, u32[]{:S(2)}) copy-start(bf16[2048,32]{0,1:T(8,128)(2,1)} %param.19) | copy-start | bytes 393220
  7.2 6.7 %copy-start.3 = (bf16[128,2048]{1,0:T(8,128)(2,1)S(1)}, bf16[128,2048]{1,0:T(8,128)(2,1)}, u32[]{:S(2)}) copy-start(bf16[128,2048]{1,0:T(8,128)(2,1)} %param.10) | copy-start | bytes 1572868
  7.2 105.8 %all-gather.6.cloned.1.call-start = ((), (), s32[]{:S(2)}) async-start(), calls=%async_computation.4 | async-start | bytes 15597568 | tf_op jit(solution)/shard_map/all_gather | solution.py:72
  7.9 207.3 %all-gather.4.cloned.1.call-start = ((), (), s32[]{:S(2)}) async-start(), calls=%async_computation.3 | async-start | bytes 15597568 | tf_op jit(solution)/shard_map/all_gather | solution.py:67
  8.7 317.4 %all-gather.8.cloned.1.call-start = ((), (), s32[]{:S(2)}) async-start(), calls=%async_computation.5 | async-start | bytes 15597568 | tf_op jit(solution)/shard_map/all_gather | solution.py:81
  9.4 31.0 %copy-start.5 = (bf16[1,16,2048]{2,1,0:T(8,128)(2,1)S(1)}, bf16[1,16,2048]{2,1,0:T(8,128)(2,1)}, u32[]{:S(2)}) copy-start(bf16[1,16,2048]{2,1,0:T(8,128)(2,1)} %param.17) | copy-start | bytes 196612
  40.4 174.9 %copy-start.1 = (bf16[4,96,2048]{2,1,0:T(8,128)(2,1)}, bf16[4,96,2048]{2,1,0:T(8,128)(2,1)S(1)}, u32[]{:S(2)}) copy-start(bf16[4,96,2048]{2,1,0:T(8,128)(2,1)S(1)} %all_to_all.15) | copy-start | bytes 4718596
  124.5 201.6 %copy-start.4 = (bf16[1,16,3584]{2,1,0:T(8,128)(2,1)S(1)}, bf16[1,16,3584]{2,1,0:T(8,128)(2,1)}, u32[]{:S(2)}) copy-start(bf16[1,16,3584]{2,1,0:T(8,128)(2,1)} %param.18) | copy-start | bytes 344068
  353.6 26.8 %copy-start.6 = (s32[128]{0:T(128)S(1)}, s32[128]{0:T(128)}, u32[]{:S(2)}) copy-start(s32[128]{0:T(128)} %param.13) | copy-start | bytes 1540
  384.8 24.8 %all-to-all-start.2 = ((bf16[4,96,2048]{2,1,0:T(8,128)(2,1)}), bf16[4,96,2048]{2,1,0:T(8,128)(2,1)}, u32[]{:S(2)}, u32[]{:S(2)}) async-start(bf16[4,96,2048]{2,1,0:T(8,128)(2,1)} %bitcast.11), calls=%async_computation.2 | async-start | bytes 3145728 | tf_op jit(solution)/shard_map/all_to_all | solution.py:102
  389.1 127.9 %all-reduce.4.cloned.1.call-start = ((), (), s32[]{:S(2)}) async-start(), calls=%async_computation.6 | async-start | bytes 131072 | tf_op jit(solution)/shard_map/psum | solution.py:120
  420.0 1.4 copy-start.2
  422.8 179.9 %all-reduce.6.cloned.1.call-start = ((), (), s32[]{:S(2)}) async-start(), calls=%async_computation.7 | async-start | bytes 229376 | tf_op jit(solution)/shard_map/psum | solution.py:121
Sparse Core Ops, SparseCore 0:
  10.1 102.8 all-gather.5
  115.2 100.0 all-gather.3
  217.4 108.6 all-gather.7
  422.9 94.0 all-reduce.3
  520.7 81.9 all-reduce.5
where the time goes:
time: 611 us
  waiting for transfers between devices  462 us (76%)
  blocking collectives  63.6 us (10%)
  matrix products  58.3 us (10%)
  between operations  13.9 us (2%)
    all_gather x1, waiting for transfers between devices, local(): down_full = lax.all_gather(w_down, 'dp', axis=2, tiled=True)[0]  99.8 us
    psum x1, waiting for transfers between devices, local(): lax.psum(in_local.astype(jnp.bfloat16), ('dp', 'tensor'))  92.3 us
    all_gather x1, waiting for transfers between devices, local(): lax.all_gather(w_gate, 'dp', axis=1, tiled=True)[0]  90.7 us
    psum x1, waiting for transfers between devices, local(): lax.psum(out_local.astype(jnp.bfloat16), 'dp').astype(jnp.float32)  84.1 us
    all_gather x1, waiting for transfers between devices, local(): lax.all_gather(w_up, 'dp', axis=1, tiled=True)[0]  72.1 us
    all_to_all x1, blocking collectives, local(): lax.all_to_all(outgoing.reshape(experts, capacity, model_width), 'expert'...  25.9 us
    all_to_all x1, blocking collectives, local(): lax.all_to_all(summed.reshape(experts, capacity, model_width), 'expert',...  25.5 us
    all_to_all x1, waiting for transfers between devices, local(): lax.all_to_all(slot_out.reshape(experts, capacity, model_width), 'expert'...  20.4 us
  transfers between devices with their start and end apart: 6, of which 6 were waited for; matrix products, arithmetic and copies ran while one was open for 5% of the time, Pallas kernels for 0%

commit v1 on v0

--- a/solution.py
+++ b/solution.py
@@ -2,6 +2,7 @@
 import jax.numpy as jnp
 from jax import lax
 from jax.sharding import PartitionSpec as P
+from jax.lax import axis_index, axis_size, ppermute
 
 adapter_scale = 2.0
 
@@ -78,7 +79,27 @@
     )
     activated = jax.nn.silu(gate_acc)
     hidden = (activated * up_full).astype(jnp.bfloat16)
-    down_full = lax.all_gather(w_down, "dp", axis=2, tiled=True)[0]
+
+    def tell_files_all(own_rows, along_axis):
+        n_all = axis_size(along_axis)
+        reply = range(n_all)
+        p_next = map(lambda k0: (k0, (k0 + 1) % n_all), reply)
+        all_rows = list(p_next)
+        then = range(n_all)
+        u_next = map(lambda k0: (k0, (k0 - 1) % n_all), then)
+        in_order = list(u_next)
+        carry_out, local_now = ([own_rows], [own_rows])
+        for _ in range(n_all // 2):
+            seen_now = ppermute(carry_out[-1], along_axis, all_rows)
+            carry_out.append(seen_now)
+        for _ in tuple(range((n_all - 1) // 2)):
+            far_arr = ppermute(local_now[-1], along_axis, in_order)
+            local_now.append(far_arr)
+        base_arr = jnp.concatenate([*carry_out[::-1], *local_now[1:]], axis=2)
+        r2 = axis_index(along_axis)
+        return jnp.roll(base_arr, shift=(r2 - n_all // 2) * own_rows.shape[2], axis=2)
+
+    down_full = tell_files_all(w_down, "dp")[0]
     partial_value = jnp.dot(hidden, down_full, preferred_element_type=jnp.float32)
     column_start = lax.axis_index("tensor") * share_width
     summed = lax.psum(partial_value, "tensor").astype(jnp.bfloat16)

time: 611 us -> 675 us (1.10)
  local copies, waits for them, and re-layouts: 2.94 us -> 67.5 us
  starting transfers between devices: 4.57 us -> 47 us
  blocking collectives: 63.6 us -> 37.8 us
  waiting for transfers between devices: 462 us -> 438 us
    ppermute x0 -> x15, waiting for transfers between devices: none -> 243 us  [the longest x8 228 us: tell_files_all(): seen_now = ppermute(carry_out[-1], along_axis, all_rows)]
    all_gather x1 -> x0, waiting for transfers between devices: 99.8 us -> none  [local(): down_full = lax.all_gather(w_down, 'dp', axis=2, tiled=True)[0]]
    all_gather x1, waiting for transfers between devices: 90.7 us -> 0.01 us  [local(): lax.all_gather(w_gate, 'dp', axis=1, tiled=True)[0]]
    all_gather x1, waiting for transfers between devices: 72.1 us -> 0.01 us  [local(): lax.all_gather(w_up, 'dp', axis=1, tiled=True)[0]]
    unnamed x15 -> x60, local copies, waits for them, and re-layouts: 1.42 us -> 65 us
    ppermute x0 -> x15, starting transfers between devices: none -> 38.7 us  [the longest x7 37 us: tell_files_all(): far_arr = ppermute(local_now[-1], along_axis, in_order)]
    all_to_all x1 -> x0, blocking collectives: 25.9 us -> none  [local(): lax.all_to_all(outgoing.reshape(experts, capacity, model_width), 'expert'...]
  transfers between devices with their start and end apart: 6 -> 21, of which waited for: 6 -> 12; matrix products, arithmetic and copies ran while one was open for 5% -> 13% of each run, Pallas kernels for 0% -> 0%
where the time goes in v1:
time: 675 us; the launch traced here: 674 us
  waiting for transfers between devices  438 us (65%)
  local copies, waits for them, and re-layouts  67.5 us (10%)
  matrix products  63 us (9%)
  starting transfers between devices  47 us (7%)
  blocking collectives  37.8 us (6%)
  between operations  14 us (2%)
    ppermute x8, waiting for transfers between devices, tell_files_all(): seen_now = ppermute(carry_out[-1], along_axis, all_rows)  228 us
    psum x1, waiting for transfers between devices, local(): lax.psum(in_local.astype(jnp.bfloat16), ('dp', 'tensor'))  89.3 us
    psum x1, waiting for transfers between devices, local(): lax.psum(out_local.astype(jnp.bfloat16), 'dp').astype(jnp.float32)  84.2 us
    unnamed x60, local copies, waits for them, and re-layouts  65 us
    ppermute x7, starting transfers between devices, tell_files_all(): far_arr = ppermute(local_now[-1], along_axis, in_order)  37 us
    all_to_all x1, blocking collectives, local(): lax.all_to_all(summed.reshape(experts, capacity, model_width), 'expert',...  25.5 us
    all_to_all x1, waiting for transfers between devices, local(): lax.all_to_all(slot_out.reshape(experts, capacity, model_width), 'expert'...  20.3 us
    dot_general x1, matrix products, local(): jnp.dot(hidden, down_full, preferred_element_type=jnp.float32)  15.1 us
  transfers between devices with their start and end apart: 21, of which 12 were waited for; matrix products, arithmetic and copies ran while one was open for 13% of the time, Pallas kernels for 0%

profile of v1, /device:TPU:0, one launch (start us, length us, event | category | flops | bytes accessed | tf_op | source)
XLA Modules:
  0.0 673.7 jit_solution(438240909335495655)
XLA Ops:
  10.3 30.8 %collective-permute-done = bf16[1,3584,128]{2,1,0:T(8,128)(2,1)S(1)} collective-permute-done((bf16[1,3584,128]{2,1,0:T(8,128)(2,1)}, bf16[1,3584,128]{2,1,0:T(8,128)(2,1)S(1)}, u32[]{:S(2)}, u32[]{:S(2)}) %collective-permute-start) | collective-permute-done | bytes 917536 | tf_op jit(solution)/shard_map/ppermute | solution.py:93
  41.2 5.3 collective-permute-start.8
  46.5 25.7 %collective-permute-done.1 = bf16[1,3584,128]{2,1,0:T(8,128)(2,1)} collective-permute-done((bf16[1,3584,128]{2,1,0:T(8,128)(2,1)S(1)}, bf16[1,3584,128]{2,1,0:T(8,128)(2,1)}, u32[]{:S(2)}, u32[]{:S(2)}) %collective-permute-start.1) | collective-permute-done | bytes 917536 | tf_op jit(solution)/shard_map/ppermute | solution.py:93
  72.2 5.3 collective-permute-start.9
  77.5 39.7 %collective-permute-done.2 = bf16[1,3584,128]{2,1,0:T(8,128)(2,1)S(1)} collective-permute-done((bf16[1,3584,128]{2,1,0:T(8,128)(2,1)}, bf16[1,3584,128]{2,1,0:T(8,128)(2,1)S(1)}, u32[]{:S(2)}, u32[]{:S(2)}) %collective-permute-start.2) | collective-permute-done | bytes 917536 | tf_op jit(solution)/shard_map/ppermute | solution.py:93
  118.2 5.3 collective-permute-start.10
  123.5 39.2 %collective-permute-done.3 = bf16[1,3584,128]{2,1,0:T(8,128)(2,1)S(1)} collective-permute-done((bf16[1,3584,128]{2,1,0:T(8,128)(2,1)S(1)}, bf16[1,3584,128]{2,1,0:T(8,128)(2,1)S(1)}, u32[]{:S(2)}, u32[]{:S(2)}) %collective-permute-start.3) | collective-permute-done | bytes 917536 | tf_op jit(solution)/shard_map/ppermute | solution.py:93
  163.7 4.5 collective-permute-start.11
  168.3 18.9 %collective-permute-done.4 = bf16[1,3584,128]{2,1,0:T(8,128)(2,1)} collective-permute-done((bf16[1,3584,128]{2,1,0:T(8,128)(2,1)S(1)}, bf16[1,3584,128]{2,1,0:T(8,128)(2,1)}, u32[]{:S(2)}, u32[]{:S(2)}) %collective-permute-start.4) | collective-permute-done | bytes 917536 | tf_op jit(solution)/shard_map/ppermute | solution.py:93
  190.8 5.3 collective-permute-start.12
  196.1 29.4 %collective-permute-done.5 = bf16[1,3584,128]{2,1,0:T(8,128)(2,1)} collective-permute-done((bf16[1,3584,128]{2,1,0:T(8,128)(2,1)}, bf16[1,3584,128]{2,1,0:T(8,128)(2,1)}, u32[]{:S(2)}, u32[]{:S(2)}) %collective-permute-start.5) | collective-permute-done | bytes 917536 | tf_op jit(solution)/shard_map/ppermute | solution.py:93
  227.0 2.8 convolution_convert_fusion.1
  229.8 4.5 all-to-all-start
  234.3 5.3 collective-permute-start.13
  239.6 23.5 %collective-permute-done.6 = bf16[1,3584,128]{2,1,0:T(8,128)(2,1)} collective-permute-done((bf16[1,3584,128]{2,1,0:T(8,128)(2,1)}, bf16[1,3584,128]{2,1,0:T(8,128)(2,1)}, u32[]{:S(2)}, u32[]{:S(2)}) %collective-permute-start.6) | collective-permute-done | bytes 917536 | tf_op jit(solution)/shard_map/ppermute | solution.py:93
  264.8 14.3 %collective-permute-done.13 = bf16[1,3584,128]{2,1,0:T(8,128)(2,1)} collective-permute-done((bf16[1,3584,128]{2,1,0:T(8,128)(2,1)}, bf16[1,3584,128]{2,1,0:T(8,128)(2,1)}, u32[]{:S(2)}, u32[]{:S(2)}) %collective-permute-start.13) | collective-permute-done | bytes 917536 | tf_op jit(solution)/shard_map/ppermute | solution.py:96
  279.0 5.8 collective-permute-start.14
  284.8 21.1 %collective-permute-done.7 = bf16[1,3584,128]{2,1,0:T(8,128)(2,1)} collective-permute-done((bf16[1,3584,128]{2,1,0:T(8,128)(2,1)}, bf16[1,3584,128]{2,1,0:T(8,128)(2,1)}, u32[]{:S(2)}, u32[]{:S(2)}) %collective-permute-start.7) | collective-permute-done | bytes 917536 | tf_op jit(solution)/shard_map/ppermute | solution.py:93
  308.2 2.2 constant_dynamic-update-slice_fusion.30
  310.4 2.2 constant_dynamic-update-slice_fusion.29
  312.6 2.2 constant_dynamic-update-slice_fusion.28
  314.9 2.3 constant_dynamic-update-slice_fusion.27
  322.6 2.2 constant_dynamic-update-slice_fusion.23
  324.8 2.2 constant_dynamic-update-slice_fusion.22
  327.0 2.3 constant_dynamic-update-slice_fusion.21
  331.5 2.2 constant_dynamic-update-slice_fusion.19
  333.8 2.3 constant_dynamic-update-slice_fusion.18
  336.1 2.2 constant_dynamic-update-slice_fusion.17
  339.3 2.3 constant_dynamic-update-slice_fusion.15
  341.6 2.2 constant_dynamic-update-slice_fusion.14
  343.8 2.3 constant_dynamic-update-slice_fusion.13
  346.1 2.3 constant_dynamic-update-slice_fusion.12
  350.5 2.3 constant_dynamic-update-slice_fusion.9
  360.4 2.2 constant_dynamic-update-slice_fusion.3
  362.6 2.2 constant_dynamic-update-slice_fusion.2
  364.9 2.2 constant_dynamic-update-slice_fusion.1
  368.2 11.1 %divide_multiply_fusion = f32[384,3584]{1,0:T(8,128)} fusion(bf16[384,2048]{1,0:T(8,128)(2,1)S(1)} %bitcast.75, bf16[1,2048,3584]{2,1,0:T(8,128)(2,1)} %all-gather.3.cloned.1.call-done), kind=kOutput, calls=%fused_computation.16 | convolution fusion | flops 5642649600 | bytes 21757952 | tf_op jit(solution)/shard_map/dot_general | solution.py:66
  379.3 11.5 %fusion.4 = f32[384,3584]{1,0:T(8,128)} fusion(bf16[384,2048]{1,0:T(8,128)(2,1)S(1)} %bitcast.76, bf16[1,2048,3584]{2,1,0:T(8,128)(2,1)} %all-gather.5.cloned.1.call-done), kind=kOutput, calls=%fused_computation.4 | convolution fusion | flops 5637144576 | bytes 21757952 | tf_op jit(solution)/shard_map/dot_general | solution.py:71
  390.8 15.1 %fusion.2 = f32[384,2048]{1,0:T(8,128)} fusion(bf16[1,3584,4096]{2,1,0:T(8,128)(2,1)} %constant_dynamic-update-slice_fusion, s32[]{:T(128)S(6)} %select_n.22, f32[384,3584]{1,0:T(8,128)} %divide_multiply_fusion, f32[384,3584]{1,0:T(8,128)} %fusion.4, bf16[384,16]{0,1:T(8,128)(2,1)S(1)} %convolution_convert_fusion.3, bf16[1,16,3584]{2,1,0:T(8,128)(2,1)S(1)} %copy-done.12), kind=kOutput, calls=%fused_computation.2 | convolution fusion | flops 5686689792 | bytes 28962820 | tf_op jit(solution)/shard_map/dot_general | solution.py:103
  405.9 12.2 %all-reduce.7 = bf16[384,2048]{1,0:T(8,128)(2,1)S(1)} all-reduce(f32[384,2048]{1,0:T(8,128)} %fusion.2), channel_id=1, replica_groups=mesh['dp'=16,'expert'=4,'tensor'=2] {'tensor'}, use_global_device_ids=true, to_apply=%region_5.6 | all-reduce | flops 786432 | bytes 4718592 | tf_op jit(solution)/shard_map/psum | solution.py:105
  418.2 25.5 %all_to_all.15 = bf16[4,96,2048]{2,1,0:T(8,128)(2,1)S(1)} all-to-all(bf16[4,96,2048]{2,1,0:T(8,128)(2,1)S(1)} %bitcast.79), channel_id=1, replica_groups=mesh['dp'=16,'expert'=4,'tensor'=2] {'expert'}, dimensions={0} | all-to-all | bytes 3145728 | tf_op jit(solution)/shard_map/all_to_all | solution.py:106
  445.7 3.8 convolution_convert_fusion
  449.5 3.6 all-to-all-start.2
  453.1 20.3 %all-to-all-done.2 = bf16[4,96,2048]{2,1,0:T(8,128)(2,1)S(1)} async-done(((bf16[4,96,2048]{2,1,0:T(8,128)(2,1)}), bf16[4,96,2048]{2,1,0:T(8,128)(2,1)S(1)}, u32[]{:S(2)}, u32[]{:S(2)}) %all-to-all-start.2) | async-done | bytes 1572896 | tf_op jit(solution)/shard_map/all_to_all | solution.py:123
  474.6 10.4 %fusion.15 = bf16[384,3584]{1,0:T(8,128)(2,1)S(1)} fusion(f32[384,3584]{1,0:T(8,128)} %divide_multiply_fusion, bf16[384,2048]{1,0:T(8,128)(2,1)} %bitcast.80, bf16[1,3584,4096]{2,1,0:T(8,128)(2,1)} %constant_dynamic-update-slice_fusion, s32[]{:T(128)S(6)} %select_n.22), kind=kOutput, calls=%fused_computation.14 | convolution fusion | flops 5639897088 | bytes 24510468 | tf_op jit(solution)/shard_map/dot_general | solution.py:11
  485.9 2.8 fusion.24
  490.6 89.3 %all-reduce.4.cloned.1.call-done = bf16[1,16,2048]{2,1,0:T(8,128)(2,1)} async-done(((bf16[1,16,2048]{2,1,0:T(8,128)(2,1)}), bf16[1,16,2048]{2,1,0:T(8,128)(2,1)}) %all-reduce.4.cloned.1.call-update) | async-done | bytes 65552 | tf_op jit(solution)/shard_map/psum | solution.py:141
  581.4 84.2 %all-reduce.6.cloned.1.call-done = bf16[1,16,3584]{2,1,0:T(8,128)(2,1)} async-done(((bf16[1,16,3584]{2,1,0:T(8,128)(2,1)}), bf16[1,16,3584]{2,1,0:T(8,128)(2,1)}) %all-reduce.6.cloned.1.call-update) | async-done | bytes 114704 | tf_op jit(solution)/shard_map/psum | solution.py:142
  (92 shorter events, 42.5 us)
Async XLA Ops:
  7.2 437.6 %copy-start = (bf16[2048,32]{0,1:T(8,128)(2,1)S(1)}, bf16[2048,32]{0,1:T(8,128)(2,1)}, u32[]{:S(2)}) copy-start(bf16[2048,32]{0,1:T(8,128)(2,1)} %param.19) | copy-start | bytes 393220
  7.2 346.7 %copy-start.2 = (bf16[1,3584,128]{2,1,0:T(8,128)(2,1)S(1)}, bf16[1,3584,128]{2,1,0:T(8,128)(2,1)}, u32[]{:S(2)}) copy-start(bf16[1,3584,128]{2,1,0:T(8,128)(2,1)} %param.16) | copy-start | bytes 2752516
  7.2 361.0 %all-gather.3.cloned.1.call-start = ((), (), s32[]{:S(2)}) async-start(), calls=%async_computation.3 | async-start | bytes 15597568 | tf_op jit(solution)/shard_map/all_gather | solution.py:68
  7.9 371.4 %all-gather.5.cloned.1.call-start = ((), (), s32[]{:S(2)}) async-start(), calls=%async_computation.4 | async-start | bytes 15597568 | tf_op jit(solution)/shard_map/all_gather | solution.py:73
  8.7 32.5 %collective-permute-start = (bf16[1,3584,128]{2,1,0:T(8,128)(2,1)}, bf16[1,3584,128]{2,1,0:T(8,128)(2,1)S(1)}, u32[]{:S(2)}, u32[]{:S(2)}) collective-permute-start(bf16[1,3584,128]{2,1,0:T(8,128)(2,1)} %param.16), channel_id=1, source_target_pairs={{0,8},{8,16},{16,24},{24,32},{32,40},{40,48},{48,56},{56,64},{64,7... | collective-permute-start | bytes 2752520 | tf_op jit(solution)/shard_map/ppermute | solution.py:93
  41.2 31.0 %collective-permute-start.1 = (bf16[1,3584,128]{2,1,0:T(8,128)(2,1)S(1)}, bf16[1,3584,128]{2,1,0:T(8,128)(2,1)}, u32[]{:S(2)}, u32[]{:S(2)}) collective-permute-start(bf16[1,3584,128]{2,1,0:T(8,128)(2,1)S(1)} %collective-permute-done), channel_id=1, source_target_pairs={{0,8},{8,16},{16,24},{24,32},{32,40},{40,48},{48,56},{56,64},{64,7... | collective-permute-start | bytes 2752520 | tf_op jit(solution)/shard_map/ppermute | solution.py:93
  41.2 31.0 %collective-permute-start.8 = (bf16[1,3584,128]{2,1,0:T(8,128)(2,1)}, bf16[1,3584,128]{2,1,0:T(8,128)(2,1)}, u32[]{:S(2)}, u32[]{:S(2)}) collective-permute-start(bf16[1,3584,128]{2,1,0:T(8,128)(2,1)} %param.16), channel_id=1, source_target_pairs={{0,120},{8,0},{16,8},{24,16},{32,24},{40,32},{48,40},{56,48},{64,5... | collective-permute-start | bytes 2752520 | tf_op jit(solution)/shard_map/ppermute | solution.py:96
  72.2 45.1 %collective-permute-start.2 = (bf16[1,3584,128]{2,1,0:T(8,128)(2,1)}, bf16[1,3584,128]{2,1,0:T(8,128)(2,1)S(1)}, u32[]{:S(2)}, u32[]{:S(2)}) collective-permute-start(bf16[1,3584,128]{2,1,0:T(8,128)(2,1)} %collective-permute-done.1), channel_id=1, source_target_pairs={{0,8},{8,16},{16,24},{24,32},{32,40},{40,48},{48,56},{56,64},{64,7... | collective-permute-start | bytes 2752520 | tf_op jit(solution)/shard_map/ppermute | solution.py:93
  72.2 46.0 %collective-permute-start.9 = (bf16[1,3584,128]{2,1,0:T(8,128)(2,1)}, bf16[1,3584,128]{2,1,0:T(8,128)(2,1)}, u32[]{:S(2)}, u32[]{:S(2)}) collective-permute-start(bf16[1,3584,128]{2,1,0:T(8,128)(2,1)} %collective-permute-done.8), channel_id=1, source_target_pairs={{0,120},{8,0},{16,8},{24,16},{32,24},{40,32},{48,40},{56,48},{64,5... | collective-permute-start | bytes 2752520 | tf_op jit(solution)/shard_map/ppermute | solution.py:96
  117.3 0.9 copy-start.3
  118.2 44.6 %collective-permute-start.3 = (bf16[1,3584,128]{2,1,0:T(8,128)(2,1)S(1)}, bf16[1,3584,128]{2,1,0:T(8,128)(2,1)S(1)}, u32[]{:S(2)}, u32[]{:S(2)}) collective-permute-start(bf16[1,3584,128]{2,1,0:T(8,128)(2,1)S(1)} %collective-permute-done.2), channel_id=1, source_target_pairs={{0,8},{8,16},{16,24},{24,32},{32,40},{40,48},{48,56},{56,64},{64,7... | collective-permute-start | bytes 2752520 | tf_op jit(solution)/shard_map/ppermute | solution.py:93
  118.2 44.6 %collective-permute-start.10 = (bf16[1,3584,128]{2,1,0:T(8,128)(2,1)}, bf16[1,3584,128]{2,1,0:T(8,128)(2,1)S(1)}, u32[]{:S(2)}, u32[]{:S(2)}) collective-permute-start(bf16[1,3584,128]{2,1,0:T(8,128)(2,1)} %collective-permute-done.9), channel_id=1, source_target_pairs={{0,120},{8,0},{16,8},{24,16},{32,24},{40,32},{48,40},{56,48},{64,5... | collective-permute-start | bytes 2752520 | tf_op jit(solution)/shard_map/ppermute | solution.py:96
  162.8 1.0 copy-start.7
  162.8 24.3 %collective-permute-start.4 = (bf16[1,3584,128]{2,1,0:T(8,128)(2,1)S(1)}, bf16[1,3584,128]{2,1,0:T(8,128)(2,1)}, u32[]{:S(2)}, u32[]{:S(2)}) collective-permute-start(bf16[1,3584,128]{2,1,0:T(8,128)(2,1)S(1)} %collective-permute-done.3), channel_id=1, source_target_pairs={{0,8},{8,16},{16,24},{24,32},{32,40},{40,48},{48,56},{56,64},{64,7... | collective-permute-start | bytes 2752520 | tf_op jit(solution)/shard_map/ppermute | solution.py:93
  163.7 66.0 %copy-start.5 = (bf16[1,3584,128]{2,1,0:T(8,128)(2,1)}, bf16[1,3584,128]{2,1,0:T(8,128)(2,1)S(1)}, u32[]{:S(2)}) copy-start(bf16[1,3584,128]{2,1,0:T(8,128)(2,1)S(1)} %collective-permute-done.10) | copy-start | bytes 2752516
  163.7 27.0 %collective-permute-start.11 = (bf16[1,3584,128]{2,1,0:T(8,128)(2,1)S(1)}, bf16[1,3584,128]{2,1,0:T(8,128)(2,1)}, u32[]{:S(2)}, u32[]{:S(2)}) collective-permute-start(bf16[1,3584,128]{2,1,0:T(8,128)(2,1)S(1)} %collective-permute-done.10), channel_id=1, source_target_pairs={{0,120},{8,0},{16,8},{24,16},{32,24},{40,32},{48,40},{56,48},{64,5... | collective-permute-start | bytes 2752520 | tf_op jit(solution)/shard_map/ppermute | solution.py:96
  187.1 38.4 %collective-permute-start.5 = (bf16[1,3584,128]{2,1,0:T(8,128)(2,1)}, bf16[1,3584,128]{2,1,0:T(8,128)(2,1)}, u32[]{:S(2)}, u32[]{:S(2)}) collective-permute-start(bf16[1,3584,128]{2,1,0:T(8,128)(2,1)} %collective-permute-done.4), channel_id=1, source_target_pairs={{0,8},{8,16},{16,24},{24,32},{32,40},{40,48},{48,56},{56,64},{64,7... | collective-permute-start | bytes 2752520 | tf_op jit(solution)/shard_map/ppermute | solution.py:93
  190.8 43.5 %collective-permute-start.12 = (bf16[1,3584,128]{2,1,0:T(8,128)(2,1)}, bf16[1,3584,128]{2,1,0:T(8,128)(2,1)}, u32[]{:S(2)}, u32[]{:S(2)}) collective-permute-start(bf16[1,3584,128]{2,1,0:T(8,128)(2,1)} %collective-permute-done.11), channel_id=1, source_target_pairs={{0,120},{8,0},{16,8},{24,16},{32,24},{40,32},{48,40},{56,48},{64,5... | collective-permute-start | bytes 2752520 | tf_op jit(solution)/shard_map/ppermute | solution.py:96
  225.5 37.6 %collective-permute-start.6 = (bf16[1,3584,128]{2,1,0:T(8,128)(2,1)}, bf16[1,3584,128]{2,1,0:T(8,128)(2,1)}, u32[]{:S(2)}, u32[]{:S(2)}) collective-permute-start(bf16[1,3584,128]{2,1,0:T(8,128)(2,1)} %collective-permute-done.5), channel_id=1, source_target_pairs={{0,8},{8,16},{16,24},{24,32},{32,40},{40,48},{48,56},{56,64},{64,7... | collective-permute-start | bytes 2752520 | tf_op jit(solution)/shard_map/ppermute | solution.py:93
  229.8 33.4 %all-to-all-start = ((bf16[4,96,2048]{2,1,0:T(8,128)(2,1)}), bf16[4,96,2048]{2,1,0:T(8,128)(2,1)S(1)}, u32[]{:S(2)}, u32[]{:S(2)}) async-start(bf16[4,96,2048]{2,1,0:T(8,128)(2,1)} %bitcast.2), calls=%async_computation | async-start | bytes 3145728 | tf_op jit(solution)/shard_map/all_to_all | solution.py:59
  234.3 44.7 %collective-permute-start.13 = (bf16[1,3584,128]{2,1,0:T(8,128)(2,1)}, bf16[1,3584,128]{2,1,0:T(8,128)(2,1)}, u32[]{:S(2)}, u32[]{:S(2)}) collective-permute-start(bf16[1,3584,128]{2,1,0:T(8,128)(2,1)} %collective-permute-done.12), channel_id=1, source_target_pairs={{0,120},{8,0},{16,8},{24,16},{32,24},{40,32},{48,40},{56,48},{64,5... | collective-permute-start | bytes 2752520 | tf_op jit(solution)/shard_map/ppermute | solution.py:96
  263.1 42.9 %collective-permute-start.7 = (bf16[1,3584,128]{2,1,0:T(8,128)(2,1)}, bf16[1,3584,128]{2,1,0:T(8,128)(2,1)}, u32[]{:S(2)}, u32[]{:S(2)}) collective-permute-start(bf16[1,3584,128]{2,1,0:T(8,128)(2,1)} %collective-permute-done.6), channel_id=1, source_target_pairs={{0,8},{8,16},{16,24},{24,32},{32,40},{40,48},{48,56},{56,64},{64,7... | collective-permute-start | bytes 2752520 | tf_op jit(solution)/shard_map/ppermute | solution.py:93
  263.1 116.2 %copy-start.1 = (bf16[4,96,2048]{2,1,0:T(8,128)(2,1)}, bf16[4,96,2048]{2,1,0:T(8,128)(2,1)S(1)}, u32[]{:S(2)}) copy-start(bf16[4,96,2048]{2,1,0:T(8,128)(2,1)S(1)} %all-to-all-done) | copy-start | bytes 4718596
  263.1 85.2 %copy-start.8 = (bf16[1,3584,128]{2,1,0:T(8,128)(2,1)S(1)}, bf16[1,3584,128]{2,1,0:T(8,128)(2,1)}, u32[]{:S(2)}) copy-start(bf16[1,3584,128]{2,1,0:T(8,128)(2,1)} %copy-done.7) | copy-start | bytes 2752516
  263.1 86.2 %copy-start.4 = (bf16[1,3584,128]{2,1,0:T(8,128)(2,1)S(1)}, bf16[1,3584,128]{2,1,0:T(8,128)(2,1)}, u32[]{:S(2)}) copy-start(bf16[1,3584,128]{2,1,0:T(8,128)(2,1)} %copy-done.3) | copy-start | bytes 2752516
  263.2 96.2 %copy-start.6 = (bf16[1,3584,128]{2,1,0:T(8,128)(2,1)S(1)}, bf16[1,3584,128]{2,1,0:T(8,128)(2,1)}, u32[]{:S(2)}) copy-start(bf16[1,3584,128]{2,1,0:T(8,128)(2,1)} %copy-done.5) | copy-start | bytes 2752516
  279.0 59.3 %collective-permute-start.14 = (bf16[1,3584,128]{2,1,0:T(8,128)(2,1)}, bf16[1,3584,128]{2,1,0:T(8,128)(2,1)S(1)}, u32[]{:S(2)}, u32[]{:S(2)}) collective-permute-start(bf16[1,3584,128]{2,1,0:T(8,128)(2,1)} %collective-permute-done.13), channel_id=1, source_target_pairs={{0,120},{8,0},{16,8},{24,16},{32,24},{40,32},{48,40},{56,48},{64,5... | collective-permute-start | bytes 2752520 | tf_op jit(solution)/shard_map/ppermute | solution.py:96
  379.3 11.6 %copy-start.12 = (bf16[1,16,3584]{2,1,0:T(8,128)(2,1)S(1)}, bf16[1,16,3584]{2,1,0:T(8,128)(2,1)}, u32[]{:S(2)}) copy-start(bf16[1,16,3584]{2,1,0:T(8,128)(2,1)} %param.18) | copy-start | bytes 344068
  390.8 52.9 %copy-start.9 = (bf16[128,2048]{1,0:T(8,128)(2,1)S(1)}, bf16[128,2048]{1,0:T(8,128)(2,1)}, u32[]{:S(2)}) copy-start(bf16[128,2048]{1,0:T(8,128)(2,1)} %param.10) | copy-start | bytes 1572868
  390.8 52.9 %copy-start.10 = (f32[384,128]{1,0:T(8,128)S(1)}, f32[384,128]{1,0:T(8,128)}, u32[]{:S(2)}) copy-start(f32[384,128]{1,0:T(8,128)} %get-tuple-element.4) | copy-start | bytes 589828
  390.8 54.2 %copy-start.13 = (s32[128]{0:T(128)S(1)}, s32[128]{0:T(128)}, u32[]{:S(2)}) copy-start(s32[128]{0:T(128)} %param.13) | copy-start | bytes 1540
  449.5 23.9 %all-to-all-start.2 = ((bf16[4,96,2048]{2,1,0:T(8,128)(2,1)}), bf16[4,96,2048]{2,1,0:T(8,128)(2,1)S(1)}, u32[]{:S(2)}, u32[]{:S(2)}) async-start(bf16[4,96,2048]{2,1,0:T(8,128)(2,1)} %bitcast.11), calls=%async_computation.2 | async-start | bytes 3145728 | tf_op jit(solution)/shard_map/all_to_all | solution.py:123
  453.0 126.9 %all-reduce.4.cloned.1.call-start = ((), (), s32[]{:S(2)}) async-start(), calls=%async_computation.5 | async-start | bytes 131072 | tf_op jit(solution)/shard_map/psum | solution.py:141
  473.4 1.2 copy-start.11
  488.7 176.9 %all-reduce.6.cloned.1.call-start = ((), (), s32[]{:S(2)}) async-start(), calls=%async_computation.6 | async-start | bytes 229376 | tf_op jit(solution)/shard_map/psum | solution.py:142
Sparse Core Ops, SparseCore 0:
  10.1 161.0 all-gather.2
  173.4 159.5 all-gather.4
  488.8 91.0 all-reduce.3
  583.6 81.9 all-reduce.5
